TPU v7x, 256 devices: a whole 4x4x8 slice. The times are simulated.
256 devices in a mesh: row: 32 (over x, z), col: 8 (over y, core).
Axes of the slice: x: 4, y: 4, z: 8, core: 2. Of those that a mesh axis runs over, the one named last changes fastest.
Arguments:
- front_tiles: bfloat16 [4, 8192, 2, 2048], P(None, 'row', None, 'col'), may hold values from -6 to 6
- fill_pattern: int32 [4, 32, 2, 8], P(None, 'row', None, 'col'), may hold values from 0 to 1
- w_inverse: bfloat16 [2, 256, 256], replicated, may hold values from -0.015625 to 0.015625
- samples: bfloat16 [4, 8192, 512], P(None, 'row'), may hold values from -6 to 6
Outputs:
- factor_slab: bfloat16 [4, 8192, 2, 2048], P(None, 'row', None, 'col')
- solved_rows: bfloat16 [4, 8192, 512], P(None, 'row')
All inputs are finite; a program needn't handle non-finite values.
Results may differ from a plain program's by a relative error of at most 0.0062.
Values may be sent and summed in bfloat16 or wider, within the bound.
No kernel may reach another device: no remote copies, remote signals or barrier semaphores. Data moves between devices by JAX's collectives and lax.ppermute only.
A program may use at most 64 MiB of HBM per device.

v0:
```python
import jax
import jax.numpy as jnp
from jax import lax
from jax.sharding import PartitionSpec as P


def broadcast(block, axis, holder):
    block = jnp.where(lax.axis_index(axis) == holder, block, jnp.zeros_like(block))
    return lax.psum(block, axis)


def share_rows(tiles, root):
    return broadcast(tiles, "col", root)


def share_samples(tiles, root):
    return broadcast(tiles, "row", root)


def column_tiles(rows, cols_here):
    row_count = lax.axis_size("row")
    col_count = lax.axis_size("col")
    col_pos = lax.axis_index("col")
    pieces = []
    for place in range(cols_here):
        wanted = place * col_count + col_pos
        holder = wanted % row_count
        local_at = wanted // row_count
        held_tile = lax.dynamic_index_in_dim(rows, local_at, 0, keepdims=False)
        pieces.append(broadcast(held_tile, "row", holder))
    return jnp.stack(pieces)


def body(front_tiles, fill_pattern, w_inverse, samples):
    rows_here = front_tiles.shape[0]
    cols_here = front_tiles.shape[2]
    row_count = lax.axis_size("row")
    row_pos = lax.axis_index("row")
    col_pos = lax.axis_index("col")
    tile_row = jnp.arange(rows_here) * row_count + row_pos
    pattern = fill_pattern.astype(jnp.bfloat16)
    masked = front_tiles * pattern
    own_first = masked[:, :, 0, :]
    first_cand = jnp.einsum(
        "akm,mn->akn", own_first, w_inverse[0], preferred_element_type=jnp.float32
    )
    first_cand = jnp.where(tile_row[:, None, None] >= 1, first_cand, 0.0).astype(jnp.bfloat16)
    first_panel = share_rows(first_cand, 0)
    first_cols = column_tiles(first_panel, cols_here)
    updated_second = own_first.astype(jnp.float32) - jnp.einsum(
        "akm,nm->akn", first_panel, first_cols[0], preferred_element_type=jnp.float32
    )
    updated_second = updated_second.astype(jnp.bfloat16)
    second_cand = jnp.einsum(
        "akm,mn->akn", updated_second, w_inverse[1], preferred_element_type=jnp.float32
    )
    second_cand = jnp.where(tile_row[:, None, None] >= 2, second_cand, 0.0).astype(jnp.bfloat16)
    second_panel = share_rows(second_cand, 1)
    second_cols = column_tiles(second_panel, cols_here)
    both_rows = jnp.concatenate([first_panel, second_panel], axis=2)
    both_cols = jnp.concatenate([first_cols, second_cols], axis=2)
    product = jnp.einsum("akm,bnm->akbn", both_rows, both_cols, preferred_element_type=jnp.float32)
    trailing = ((masked.astype(jnp.float32) - product) * pattern.astype(jnp.float32)).astype(
        jnp.bfloat16
    )
    first_lead = jnp.where(tile_row[:, None, None] >= 1, first_panel, own_first)
    second_lead = jnp.where(tile_row[:, None, None] >= 2, second_panel, updated_second)
    lead_tiles = jnp.where(
        col_pos == 0, first_lead, jnp.where(col_pos == 1, second_lead, trailing[:, :, 0, :])
    )
    factor_slab = trailing.at[:, :, 0, :].set(lead_tiles)
    first_local = jnp.einsum(
        "mn,ms->ns", w_inverse[0], samples[0], preferred_element_type=jnp.float32
    )
    first_solve = share_samples(first_local.astype(jnp.bfloat16), 0)
    reduced = (
        samples[0].astype(jnp.float32)
        - jnp.dot(first_panel[0], first_solve, preferred_element_type=jnp.float32)
    ).astype(jnp.bfloat16)
    second_local = jnp.einsum(
        "mn,ms->ns", w_inverse[1], reduced, preferred_element_type=jnp.float32
    )
    second_solve = share_samples(second_local.astype(jnp.bfloat16), 1)
    stacked = jnp.concatenate([first_solve, second_solve], axis=0)
    remaining = samples.astype(jnp.float32) - jnp.einsum(
        "akm,ms->aks", both_rows, stacked, preferred_element_type=jnp.float32
    )
    remaining = remaining.astype(jnp.bfloat16)
    top_rows = jnp.where(
        row_pos == 0, first_solve, jnp.where(row_pos == 1, second_solve, remaining[0])
    )
    solved_rows = remaining.at[0].set(top_rows)
    return (factor_slab, solved_rows)


def solution(mesh):
    in_specs = (P(None, "row", None, "col"), P(None, "row", None, "col"), P(), P(None, "row", None))
    out_specs = (P(None, "row", None, "col"), P(None, "row", None))
    return jax.shard_map(body, mesh=mesh, in_specs=in_specs, out_specs=out_specs, check_vma=False)
```

profile of v0, /device:TPU:8, one launch (start us, length us, event | category | flops | bytes accessed | tf_op | source)
XLA Modules:
  0.0 465.0 jit_solution(3660325440382189734)
XLA Ops:
  7.2 0.0 all-reduce.7.cloned.1.call-start
  7.2 0.7 convert_element_type.41
  7.9 0.0 copy-start.8
  7.9 1.4 copy_multiply_fusion
  9.4 0.0 copy-done.8
  9.4 0.0 copy-start.6
  9.4 1.1 fusion.4
  10.5 0.0 all-reduce.7.cloned.1.call-update
  10.5 0.0 all-reduce.13.cloned.1.call-start
  10.6 0.0 copy-done.6
  10.6 1.0 fusion.6
  11.6 66.2 %all-reduce.7.cloned.1.call-done = bf16[4,256,256]{2,1,0:T(8,128)(2,1)} async-done(((bf16[4,256,256]{2,1,0:T(8,128)(2,1)}), bf16[4,256,256]{2,1,0:T(8,128)(2,1)}) %all-reduce.7.cloned.1.call-update) | async-done | bytes 524304 | tf_op jit(solution)/shard_map/psum | solution.py:9
  77.8 0.0 copy-start
  77.8 1.8 dynamic-slice_select_fusion.2
  79.5 0.0 all-reduce.13.cloned.1.call-update
  79.6 0.0 all-reduce.9.cloned.1.call-start
  79.6 150.6 %all-reduce.13.cloned.1.call-done = (bf16[256,256]{1,0:T(8,128)(2,1)}, bf16[256,512]{1,0:T(8,128)(2,1)}) async-done(((bf16[256,256]{1,0:T(8,128)(2,1)}, bf16[256,512]{1,0:T(8,128)(2,1)}), (bf16[256,256]{1,0:T(8,128)(2,1)}, bf16[256,512]{1,0:T(8,128)(2,1)})) %all-reduce.13.cloned.1.call-update) | async-done | bytes 393232 | tf_op jit(solution)/shard_map/psum | solution.py:9
  230.3 0.0 copy-done
  230.3 1.2 fusion
  231.5 0.0 copy-start.2
  231.5 2.0 fusion.3
  233.6 0.0 all-reduce.9.cloned.1.call-update
  233.6 0.0 all-reduce.11.cloned.1.call-start
  233.6 0.0 copy-done.2
  233.6 2.1 fusion.8
  235.7 59.4 %all-reduce.9.cloned.1.call-done = bf16[4,256,256]{2,1,0:T(8,128)(2,1)} async-done(((bf16[4,256,256]{2,1,0:T(8,128)(2,1)}), bf16[4,256,256]{2,1,0:T(8,128)(2,1)}) %all-reduce.9.cloned.1.call-update) | async-done | bytes 524304 | tf_op jit(solution)/shard_map/psum | solution.py:9
  295.1 0.0 copy-start.1
  295.1 1.8 dynamic-slice_select_fusion.1
  296.9 0.0 all-reduce.11.cloned.1.call-update
  296.9 0.0 copy-start.4
  296.9 0.8 constant_dynamic-update-slice_fusion.1
  297.7 0.0 copy-done.1
  297.7 0.8 constant_dynamic-update-slice_fusion
  298.6 152.2 %all-reduce.11.cloned.1.call-done = (bf16[1,256,256]{2,1,0:T(8,128)(2,1)}, bf16[1,256,256]{2,1,0:T(8,128)(2,1)}, bf16[1,256,256]{2,1,0:T(8,128)(2,1)}, bf16[256,512]{1,0:T(8,128)(2,1)}) async-done(((bf16[1,256,256]{2,1,0:T(8,128)(2,1)}, bf16[1,256,256]{2,1,0:T(8,128)(2,1)}, bf16[1,256,256]{2,1,0:T(8,128)(2,1)}, bf16[256,512]{1,0:T(8,128)(2,1)}), (bf16[1,256,256]{2,1,0:T(8,128)(2,1)}, ...) | async-done | bytes 655376 | tf_op jit(solution)/shard_map/psum | solution.py:9
  450.7 0.0 copy-done.4
  450.7 2.1 multiply_convert_fusion
  452.8 0.6 fusion.13
  453.4 0.0 copy-start.3
  453.4 0.0 copy-start.7
  453.4 2.0 copy.9
  455.5 0.0 copy-done.3
  455.5 0.0 copy-done.7
  455.5 1.9 subtract_convert_fusion
  457.4 0.1 fusion.26
  457.5 0.0 copy-start.5
  457.6 1.0 copy-done.5
  (3 shorter events, 0.0 us)
Async XLA Ops:
  7.2 70.6 %all-reduce.7.cloned.1.call-start = ((), (), s32[]{:S(2)}) async-start(), calls=%async_computation | async-start | bytes 1048576 | tf_op jit(solution)/shard_map/psum | solution.py:9
  7.9 1.4 copy-start.8
  9.4 1.2 copy-start.6
  10.5 219.8 %all-reduce.13.cloned.1.call-start = ((), (), s32[]{:S(2)}) async-start(), calls=%async_computation.3 | async-start | bytes 786432 | tf_op jit(solution)/shard_map/psum | solution.py:9
  77.8 152.5 %copy-start = (bf16[4,256,256]{2,1,0:T(8,128)(2,1)S(1)}, bf16[4,256,256]{2,1,0:T(8,128)(2,1)}, u32[]{:S(2)}) copy-start(bf16[4,256,256]{2,1,0:T(8,128)(2,1)} %all-reduce.7.cloned.1.call-done) | copy-start | bytes 1572868
  79.6 215.6 %all-reduce.9.cloned.1.call-start = ((), (), s32[]{:S(2)}) async-start(), calls=%async_computation.1 | async-start | bytes 1048576 | tf_op jit(solution)/shard_map/psum | solution.py:9
  231.5 2.1 copy-start.2
  233.6 217.2 %all-reduce.11.cloned.1.call-start = ((), (), s32[]{:S(2)}) async-start(), calls=%async_computation.2 | async-start | bytes 1310720 | tf_op jit(solution)/shard_map/psum | solution.py:9
  295.1 2.6 copy-start.1
  296.9 153.9 %copy-start.4 = (bf16[256,256]{1,0:T(8,128)(2,1)S(1)}, bf16[256,256]{1,0:T(8,128)(2,1)}, u32[]{:S(2)}) copy-start(bf16[256,256]{1,0:T(8,128)(2,1)} %get-tuple-element.32) | copy-start | bytes 393220
  453.4 2.1 copy-start.3
  453.4 2.1 copy-start.7
  457.5 1.0 copy-start.5
Sparse Core Ops, SparseCore 0:
  10.9 66.8 all-reduce.6
  81.9 148.3 all-reduce.12
  233.7 61.3 all-reduce.8
  299.3 151.3 all-reduce.10
where the time goes:
time: 465 us
  waiting for transfers between devices  429 us (92%)
  between operations  13.9 us (3%)
  matrix products  11.4 us (2%)
  other arithmetic  6.38 us (1%)
  local copies, waits for them, and re-layouts  4.71 us (1%)
    psum x4, waiting for transfers between devices, broadcast(): return lax.psum(block, axis)  428 us
  transfers between devices with their start and end apart: 4, of which 4 were waited for; matrix products, arithmetic and copies ran while one was open for 1% of the time, Pallas kernels for 0%

commit v1 on v0

--- a/solution.py
+++ b/solution.py
@@ -4,9 +4,15 @@
 from jax.sharding import PartitionSpec as P
 
 
+def add_all(block, mesh_axis):
+    pieces = lax.all_gather(block, mesh_axis, axis=0, tiled=False)
+    acc = pieces.sum(axis=0)
+    return acc
+
+
 def broadcast(block, axis, holder):
     block = jnp.where(lax.axis_index(axis) == holder, block, jnp.zeros_like(block))
-    return lax.psum(block, axis)
+    return add_all(block, axis)
 
 
 def share_rows(tiles, root):

time: 465 us -> 642 us (1.38)
  waiting for transfers between devices: 429 us -> 573 us
  other arithmetic: 6.38 us -> 33.2 us
  local copies, waits for them, and re-layouts: 4.71 us -> 12.7 us
    all_gather x0 -> x8, waiting for transfers between devices: none -> 571 us  [add_all(): pieces = lax.all_gather(block, mesh_axis, axis=0, tiled=False)]
    psum x4 -> x0, waiting for transfers between devices: 428 us -> none  [broadcast(): return lax.psum(block, axis)]
    reduce_sum x0 -> x8, other arithmetic: none -> 28.9 us  [add_all(): acc = pieces.sum(axis=0)]
    unnamed x20 -> x8, local copies, waits for them, and re-layouts: 3.88 us -> 12.6 us
  transfers between devices with their start and end apart: 4 -> 8, of which waited for: 4 -> 8; matrix products, arithmetic and copies ran while one was open for 1% -> 4% of each run, Pallas kernels for 0% -> 0%
where the time goes in v1:
time: 642 us; the launch traced here: 641 us
  waiting for transfers between devices  573 us (89%)
  other arithmetic  33.2 us (5%)
  between operations  14.3 us (2%)
  local copies, waits for them, and re-layouts  12.7 us (2%)
  matrix products  8.02 us (1%)
    all_gather x8, waiting for transfers between devices, add_all(): pieces = lax.all_gather(block, mesh_axis, axis=0, tiled=False)  571 us
    reduce_sum x8, other arithmetic, add_all(): acc = pieces.sum(axis=0)  28.9 us
  transfers between devices with their start and end apart: 8, of which 8 were waited for; matrix products, arithmetic and copies ran while one was open for 4% of the time, Pallas kernels for 0%

profile of v1, /device:TPU:8, one launch (start us, length us, event | category | flops | bytes accessed | tf_op | source)
XLA Modules:
  0.0 641.3 jit_solution(4651787603233146712)
XLA Ops:
  7.2 0.0 copy-start.2
  7.2 0.0 all-gather.21.cloned.1.call-start
  7.2 0.7 convert_element_type.27
  8.0 1.4 copy_multiply_fusion
  9.3 0.0 copy-done.2
  9.4 1.1 fusion.4
  10.4 0.0 all-gather.21.cloned.1.call-update
  10.5 0.0 all-gather.13.cloned.1.call-start
  10.6 36.5 %all-gather.21.cloned.1.call-done = bf16[32,256,256]{2,1,0:T(8,128)(2,1)} async-done(((bf16[4,256,256]{2,1,0:T(8,128)(2,1)}), bf16[32,256,256]{2,1,0:T(8,128)(2,1)}) %all-gather.21.cloned.1.call-update) | async-done | bytes 4194320 | tf_op jit(solution)/shard_map/all_gather | solution.py:8
  47.1 2.8 reduce_sum.100
  50.0 0.7 dynamic-slice_select_fusion.2
  50.7 0.0 all-gather.13.cloned.1.call-update
  50.7 0.0 all-gather.23.cloned.1.call-start
  50.8 82.8 %all-gather.13.cloned.1.call-done = bf16[32,256,256]{2,1,0:T(8,128)(2,1)} async-done(((bf16[1,256,256]{2,1,0:T(8,128)(2,1)}), bf16[32,256,256]{2,1,0:T(8,128)(2,1)}) %all-gather.13.cloned.1.call-update) | async-done | bytes 4194320 | tf_op jit(solution)/shard_map/all_gather | solution.py:8
  133.6 2.8 reduce_sum.101
  136.4 0.3 fusion
  136.7 1.1 fusion.3
  137.8 0.0 all-gather.23.cloned.1.call-update
  137.8 0.0 all-gather.25.cloned.1.call-start
  137.9 1.9 fusion.6
  139.8 0.0 all-gather.25.cloned.1.call-update
  139.8 0.0 all-gather.15.cloned.1.call-start
  139.8 0.5 all-gather.15.cloned.1.call-update
  140.4 0.0 all-gather.17.cloned.1.call-start
  140.4 27.9 %all-gather.23.cloned.1.call-done = bf16[32,256,256]{2,1,0:T(8,128)(2,1)} async-done(((bf16[4,256,256]{2,1,0:T(8,128)(2,1)}), bf16[32,256,256]{2,1,0:T(8,128)(2,1)}) %all-gather.23.cloned.1.call-update) | async-done | bytes 4194320 | tf_op jit(solution)/shard_map/all_gather | solution.py:8
  168.3 2.8 reduce_sum.102
  171.2 0.7 dynamic-slice_select_fusion.1
  171.9 0.0 all-gather.17.cloned.1.call-update
  171.9 0.0 all-gather.19.cloned.1.call-start
  172.0 0.7 all-gather.19.cloned.1.call-update
  172.7 0.2 all-gather.27.cloned.1.call-start
  172.9 97.2 %all-gather.25.cloned.1.call-done = bf16[8192,512]{1,0:T(8,128)(2,1)} async-done(((bf16[256,512]{1,0:T(8,128)(2,1)}), bf16[8192,512]{1,0:T(8,128)(2,1)}) %all-gather.25.cloned.1.call-update) | async-done | bytes 8388624 | tf_op jit(solution)/shard_map/all_gather | solution.py:8
  270.2 4.8 reduce_sum.106
  274.9 2.2 fusion.8
  277.1 0.0 all-gather.27.cloned.1.call-update
  277.1 74.3 %all-gather.15.cloned.1.call-done = bf16[32,256,256]{2,1,0:T(8,128)(2,1)} async-done(((bf16[1,256,256]{2,1,0:T(8,128)(2,1)}), bf16[32,256,256]{2,1,0:T(8,128)(2,1)}) %all-gather.15.cloned.1.call-update) | async-done | bytes 4194320 | tf_op jit(solution)/shard_map/all_gather | solution.py:8
  351.4 2.8 reduce_sum.103
  354.2 78.2 %all-gather.17.cloned.1.call-done = bf16[32,256,256]{2,1,0:T(8,128)(2,1)} async-done(((bf16[1,256,256]{2,1,0:T(8,128)(2,1)}), bf16[32,256,256]{2,1,0:T(8,128)(2,1)}) %all-gather.17.cloned.1.call-update) | async-done | bytes 4194320 | tf_op jit(solution)/shard_map/all_gather | solution.py:8
  432.4 2.8 reduce_sum.104
  435.2 78.3 %all-gather.19.cloned.1.call-done = bf16[32,256,256]{2,1,0:T(8,128)(2,1)} async-done(((bf16[1,256,256]{2,1,0:T(8,128)(2,1)}), bf16[32,256,256]{2,1,0:T(8,128)(2,1)}) %all-gather.19.cloned.1.call-update) | async-done | bytes 4194320 | tf_op jit(solution)/shard_map/all_gather | solution.py:8
  513.5 2.8 reduce_sum.105
  516.3 0.7 multiply_convert_fusion
  517.1 0.5 fusion.13
  517.6 2.0 copy.13
  519.7 95.9 %all-gather.27.cloned.1.call-done = bf16[8192,512]{0,1:T(8,128)(2,1)} async-done(((bf16[256,512]{0,1:T(8,128)(2,1)}), bf16[8192,512]{0,1:T(8,128)(2,1)}) %all-gather.27.cloned.1.call-update) | async-done | bytes 8388624 | tf_op jit(solution)/shard_map/all_gather | solution.py:8
  615.6 9.5 %copy.17 = bf16[64,8,32,256]{3,2,1,0:T(8,128)(2,1)} copy(bf16[64,8,32,256]{3,1,2,0:T(8,128)(2,1)} %bitcast.83) | data formatting | bytes 16777216
  625.2 0.0 copy-start.1
  625.2 7.3 %bitcast_reduce_fusion = bf16[256,512]{0,1:T(8,128)(2,1)S(1)} fusion(bf16[64,8,32,256]{3,2,1,0:T(8,128)(2,1)} %copy.17), kind=kLoop, calls=%fused_computation | loop fusion | flops 4063232 | bytes 8650752 | tf_op jit(solution)/shard_map/reduce_sum | solution.py:9
  632.4 0.1 copy.11
  632.6 0.0 copy-done.1
  632.6 0.7 subtract_convert_fusion
  633.3 0.1 fusion.24
  633.5 0.0 copy-start
  633.5 1.0 copy-done
  (3 shorter events, 0.0 us)
Async XLA Ops:
  7.2 2.2 copy-start.2
  7.2 39.9 %all-gather.21.cloned.1.call-start = ((), (), s32[]{:S(2)}) async-start(), calls=%async_computation.4 | async-start | bytes 4718592 | tf_op jit(solution)/shard_map/all_gather | solution.py:8
  10.5 123.1 %all-gather.13.cloned.1.call-start = ((), (), s32[]{:S(2)}) async-start(), calls=%async_computation | async-start | bytes 4325376 | tf_op jit(solution)/shard_map/all_gather | solution.py:8
  50.7 117.6 %all-gather.23.cloned.1.call-start = ((), (), s32[]{:S(2)}) async-start(), calls=%async_computation.5 | async-start | bytes 4718592 | tf_op jit(solution)/shard_map/all_gather | solution.py:8
  137.8 132.4 %all-gather.25.cloned.1.call-start = ((), (), s32[]{:S(2)}) async-start(), calls=%async_computation.6 | async-start | bytes 8650752 | tf_op jit(solution)/shard_map/all_gather | solution.py:8
  139.8 211.7 %all-gather.15.cloned.1.call-start = ((), (), s32[]{:S(2)}) async-start(), calls=%async_computation.1 | async-start | bytes 4325376 | tf_op jit(solution)/shard_map/all_gather | solution.py:8
  140.4 292.0 %all-gather.17.cloned.1.call-start = ((), (), s32[]{:S(2)}) async-start(), calls=%async_computation.2 | async-start | bytes 4325376 | tf_op jit(solution)/shard_map/all_gather | solution.py:8
  171.9 341.6 %all-gather.19.cloned.1.call-start = ((), (), s32[]{:S(2)}) async-start(), calls=%async_computation.3 | async-start | bytes 4325376 | tf_op jit(solution)/shard_map/all_gather | solution.py:8
  172.7 442.9 %all-gather.27.cloned.1.call-start = ((), (), s32[]{:S(2)}) async-start(), calls=%async_computation.7 | async-start | bytes 8650752 | tf_op jit(solution)/shard_map/all_gather | solution.py:8
  625.2 7.4 %copy-start.1 = (bf16[4,256,512]{2,1,0:T(8,128)(2,1)S(1)}, bf16[4,256,512]{2,1,0:T(8,128)(2,1)}, u32[]{:S(2)}) copy-start(bf16[4,256,512]{2,1,0:T(8,128)(2,1)} %param.11) | copy-start | bytes 3145732
  633.5 1.0 copy-start
Sparse Core Ops, SparseCore 0:
  10.6 36.4 all-gather.20
  50.8 82.6 all-gather.12
  137.9 30.3 all-gather.22
  171.4 98.7 all-gather.24
  272.6 78.7 all-gather.14
  353.9 78.4 all-gather.16
  435.0 78.4 all-gather.18
  516.6 99.0 all-gather.26
